TPU v7x, 32 devices: a whole 2x2x4 slice. The times are simulated.
32 devices in a mesh: col: 4 (over y, x), row: 8 (over z, core).
Axes of the slice: x: 2, y: 2, z: 4, core: 2. Of those that a mesh axis runs over, the one named last changes fastest.
Arguments:
- weights: float32 [16384, 16384], P('row', 'col'), may hold values from -6 to 6
- factor_rows: bfloat16 [1024, 16384], P('row', 'col'), may hold values from -0.25 to 0.25
- diag_inverse: bfloat16 [8, 128, 128], replicated, as said below
- prune_tiles: int32 [128, 8], P('row'), may hold values 0 or 1
- pivot_order: int32 [8], replicated, may hold values from 0 to 127, as said below
Outputs:
- pruned_weights: float32 [16384, 16384], P('row', 'col')
Inputs may be any that keep to these rules, and one draw needn't show every extreme that they name: `pivot_order`: the 8 block numbers are distinct; block 0 and the last block are among them. `diag_inverse`: each block is upper triangular with positive diagonal.
All inputs are finite; a program needn't handle non-finite values. No bound on the sum of `prune_tiles` on one device may be relied on, other than what follows from the above.
Results may differ from a plain program's by a relative error of at most 0.0003.
Values may be sent and summed in bfloat16 or wider, within the bound.
No kernel may reach another device: no remote copies, remote signals or barrier semaphores. Data moves between devices by JAX's collectives and lax.ppermute only.
A program may use at most 192 MiB of HBM per device.

v0:
```python
import jax
import jax.numpy as jnp
from jax import lax
from jax.sharding import PartitionSpec as P

BLOCK = 128
PIVOTS = 8


def shards(weights, factor_rows, diag_inverse, prune_tiles, pivot_order):
    cols_local = weights.shape[1]
    blocks_dev = cols_local // BLOCK
    col_index = lax.axis_index("col")
    factor_all = lax.all_gather(factor_rows, "row", axis=0, tiled=True)
    pruned_all = jnp.repeat(prune_tiles.astype(jnp.float32), BLOCK, axis=0)
    panel_parts = []
    factor_parts = []
    start_list = []
    owner_list = []
    for step in range(PIVOTS):
        block_id = pivot_order[step]
        owner_col = block_id // blocks_dev
        local_start = block_id % blocks_dev * BLOCK
        owned = (owner_col == col_index).astype(jnp.float32)
        panel_parts.append(lax.dynamic_slice_in_dim(weights, local_start, BLOCK, 1) * owned)
        factor_parts.append(
            lax.dynamic_slice_in_dim(factor_all, local_start, BLOCK, 1).astype(jnp.float32) * owned
        )
        start_list.append(local_start)
        owner_list.append(owner_col)
    panel_local = jnp.concatenate(panel_parts, axis=1)
    factor_local = jnp.concatenate(factor_parts, axis=1)
    panels, factor_pivots = lax.psum((panel_local, factor_local), "col")
    error_list = []
    stored_list = []
    for step in range(PIVOTS):
        panel_now = panels[:, step * BLOCK : (step + 1) * BLOCK]
        if step > 0:
            stacked = jnp.concatenate(error_list, axis=1)
            factor_slice = factor_pivots[: step * BLOCK, step * BLOCK : (step + 1) * BLOCK]
            panel_now = panel_now - jnp.dot(stacked, factor_slice, precision=lax.Precision.HIGHEST)
        pruned = pruned_all[:, step : step + 1]
        errors = (
            jnp.dot(
                panel_now, diag_inverse[step].astype(jnp.float32), precision=lax.Precision.HIGHEST
            )
            * pruned
        )
        error_list.append(errors)
        stored_list.append(panel_now * (1.0 - pruned))
    stacked = jnp.concatenate(error_list, axis=1)
    total = jnp.dot(stacked, factor_all.astype(jnp.float32), precision=lax.Precision.HIGHEST)
    current = weights - total
    for step in range(PIVOTS):
        old_slice = lax.dynamic_slice_in_dim(current, start_list[step], BLOCK, 1)
        new_slice = jnp.where(owner_list[step] == col_index, stored_list[step], old_slice)
        current = lax.dynamic_update_slice_in_dim(current, new_slice, start_list[step], 1)
    return current


def solution(mesh):
    return jax.shard_map(
        shards,
        mesh=mesh,
        in_specs=(P("row", "col"), P("row", "col"), P(), P("row", None), P()),
        out_specs=P("row", "col"),
        check_vma=False,
    )
```

profile of v0, /device:TPU:0, one launch (start us, length us, event | category | flops | bytes accessed | tf_op | source)
XLA Modules:
  0.0 507.3 jit_solution(12240714355730047815)
XLA Ops:
  6.5 0.7 all-gather.2.cloned.1.call-update
  7.3 0.0 all-reduce.3.cloned.1.call-start
  7.3 1.6 fusion.51
  29.3 2.3 multiply_dynamic-update-slice_fusion.7
  31.6 2.3 multiply_dynamic-update-slice_fusion.6
  33.8 2.3 multiply_dynamic-update-slice_fusion.5
  36.1 2.3 multiply_dynamic-update-slice_fusion.4
  38.4 2.3 multiply_dynamic-update-slice_fusion.3
  40.6 2.3 multiply_dynamic-update-slice_fusion.2
  42.9 2.3 multiply_dynamic-update-slice_fusion.1
  45.2 2.3 multiply_dynamic-update-slice_fusion
  47.4 46.3 %all-gather.2.cloned.1.call-done = bf16[1024,4096]{1,0:T(8,128)(2,1)} async-done(((bf16[128,4096]{1,0:T(8,128)(2,1)}), bf16[1024,4096]{1,0:T(8,128)(2,1)}) %all-gather.2.cloned.1.call-update) | async-done | bytes 8388624 | tf_op jit(solution)/shard_map/all_gather | solution.py:14
  93.7 1.8 multiply_dynamic-update-slice_fusion.15
  95.5 1.8 multiply_dynamic-update-slice_fusion.14
  97.4 1.8 multiply_dynamic-update-slice_fusion.13
  99.2 1.8 multiply_dynamic-update-slice_fusion.12
  101.0 1.8 multiply_dynamic-update-slice_fusion.11
  102.8 1.8 multiply_dynamic-update-slice_fusion.10
  104.6 1.9 multiply_dynamic-update-slice_fusion.9
  106.5 1.9 multiply_dynamic-update-slice_fusion.8
  108.4 0.1 copy.7
  108.5 0.1 broadcast_bitcast_fusion
  108.5 0.1 broadcast_subtract_fusion
  108.6 237.7 %all-reduce.3.cloned.1.call-done = (f32[2048,1024]{1,0:T(8,128)}, f32[1024,1024]{1,0:T(8,128)}) async-done(((f32[2048,1024]{1,0:T(8,128)}, f32[1024,1024]{1,0:T(8,128)}), (f32[2048,1024]{1,0:T(8,128)}, f32[1024,1024]{1,0:T(8,128)})) %all-reduce.3.cloned.1.call-update) | async-done | bytes 12582928 | tf_op jit(solution)/shard_map/psum | solution.py:33
  346.3 3.2 constant_dynamic-update-slice_fusion.17
  349.5 3.2 convolution_subtract_fusion.5
  352.8 1.9 constant_dynamic-update-slice_fusion.16
  354.6 4.4 convolution_subtract_fusion.4
  359.1 1.9 constant_dynamic-update-slice_fusion.15
  360.9 6.8 %fusion.14 = f32[2048,128]{1,0:T(8,128)S(1)} fusion(f32[2048,128]{0,1:T(8,128)S(1)} %get-tuple-element.58, f32[2048,128]{0,1:T(8,128)S(1)} %get-tuple-element.57, f32[2048,128]{0,1:T(8,128)S(1)} %get-tuple-element.56, f32[2048,1024]{1,0:T(8,128)S(1)} %bitcast.78, f32[1024,1024]{1,0:T(8,128)} %get-tuple-element.6), kind=kOutput, calls=%fused_computation.16 | convolution fusion | flops 1209794560 | bytes 5439488 | tf_op jit(solution)/shard_map/dot_general | solution.py:41
  367.7 1.9 constant_dynamic-update-slice_fusion.14
  369.6 7.9 %fusion.18 = f32[2048,128]{1,0:T(8,128)S(1)} fusion(f32[2048,128]{0,1:T(8,128)S(1)} %get-tuple-element.59, f32[2048,128]{0,1:T(8,128)S(1)} %get-tuple-element.58, f32[2048,128]{0,1:T(8,128)S(1)} %get-tuple-element.57, f32[2048,128]{0,1:T(8,128)S(1)} %get-tuple-element.56, f32[2048,1024]{1,0:T(8,128)S(1)} %bitcast.78, f32[1024,1024]{1,0:T(8,128)} %get-tuple-element.6), kind=kOutput, calls=%fused_computation.30 | convolution fusion | flops 1614020608 | bytes 6553600 | tf_op jit(solution)/shard_map/dot_general | solution.py:41
  377.5 1.8 constant_dynamic-update-slice_fusion.13
  379.3 9.9 %convolution_subtract_fusion.3 = f32[2048,128]{1,0:T(8,128)S(1)} fusion(f32[2048,640]{0,1:T(8,128)S(1)} %get-tuple-element.15, f32[2048,1024]{1,0:T(8,128)S(1)} %bitcast.78, f32[1024,1024]{1,0:T(8,128)} %get-tuple-element.6), kind=kOutput, calls=%fused_computation.18 | convolution fusion | flops 2013528064 | bytes 7667712 | tf_op jit(solution)/shard_map/dot_general | solution.py:41
  389.2 1.8 constant_dynamic-update-slice_fusion.12
  391.0 11.5 %convolution_subtract_fusion.1 = f32[2048,128]{1,0:T(8,128)S(1)} fusion(f32[2048,768]{0,1:T(8,128)S(1)} %get-tuple-element.11, f32[2048,1024]{1,0:T(8,128)S(1)} %bitcast.78, f32[1024,1024]{1,0:T(8,128)} %get-tuple-element.6), kind=kOutput, calls=%fused_computation.15 | convolution fusion | flops 2416181248 | bytes 8781824 | tf_op jit(solution)/shard_map/dot_general | solution.py:41
  402.4 1.7 constant_dynamic-update-slice_fusion.11
  404.1 13.4 %convolution_subtract_fusion.2 = f32[2048,128]{1,0:T(8,128)S(1)} fusion(f32[2048,896]{0,1:T(8,128)S(1)} %get-tuple-element.7, f32[2048,1024]{1,0:T(8,128)S(1)} %bitcast.78, f32[1024,1024]{1,0:T(8,128)} %get-tuple-element.6), kind=kOutput, calls=%fused_computation.17 | convolution fusion | flops 2818834432 | bytes 9895936 | tf_op jit(solution)/shard_map/dot_general | solution.py:41
  417.5 1.7 fusion.17
  419.3 60.7 %convolution_subtract_fusion = f32[2048,4096]{1,0:T(8,128)} fusion(f32[2048,4096]{1,0:T(8,128)} %param.5, f32[2048,1024]{0,1:T(8,128)} %fusion.17, bf16[1024,4096]{1,0:T(8,128)(2,1)} %all-gather.2.cloned.1.call-done), kind=kOutput, calls=%fused_computation | convolution fusion | flops 103087603712 | bytes 83886080 | tf_op jit(solution)/shard_map/dot_general | solution.py:52
  479.9 2.6 select_dynamic-update-slice_fusion.7
  482.5 2.5 select_dynamic-update-slice_fusion.6
  485.0 2.5 select_dynamic-update-slice_fusion.5
  487.6 2.5 select_dynamic-update-slice_fusion.4
  490.1 2.5 select_dynamic-update-slice_fusion.3
  492.6 2.5 select_dynamic-update-slice_fusion.2
  495.2 2.5 select_dynamic-update-slice_fusion.1
  497.7 2.5 select_dynamic-update-slice_fusion
  (12 shorter events, 0.0 us)
Async XLA Ops:
  6.5 87.2 %all-gather.2.cloned.1.call-start = ((), (), s32[]{:S(2)}) async-start(), calls=%async_computation | async-start | bytes 9437184 | tf_op jit(solution)/shard_map/all_gather | solution.py:14
  7.3 339.0 %all-reduce.3.cloned.1.call-start = ((), (), s32[]{:S(2)}) async-start(), calls=%async_computation.1 | async-start | bytes 25165824 | tf_op jit(solution)/shard_map/psum | solution.py:33
  102.8 5.6 %copy-start.1 = (s32[16,8]{0,1:T(8,128)S(1)}, s32[16,8]{0,1:T(8,128)}, u32[]{:S(2)}) copy-start(s32[16,8]{0,1:T(8,128)} %param.8) | copy-start | bytes 1540
  104.6 241.7 %copy-start = (bf16[8,128,128]{2,1,0:T(8,128)(2,1)S(1)}, bf16[8,128,128]{2,1,0:T(8,128)(2,1)}, u32[]{:S(2)}) copy-start(bf16[8,128,128]{2,1,0:T(8,128)(2,1)} %param.7) | copy-start | bytes 786436
  346.3 8.3 %slice-start = ((s8[8388608]{0:T(1024)(128)(4,1)}), s8[4194304]{0:T(1024)(128)(4,1)S(1)}, s32[]{:S(2)}) async-start(s8[8388608]{0:T(1024)(128)(4,1)} %bitcast.77), calls=%async_computation.2 | async-start | bytes 8388608
  349.5 5.1 %slice-start.1 = ((s8[8388608]{0:T(1024)(128)(4,1)}), s8[4194304]{0:T(1024)(128)(4,1)S(1)}, s32[]{:S(2)}) async-start(s8[8388608]{0:T(1024)(128)(4,1)} %bitcast.77), calls=%async_computation.3 | async-start | bytes 8388608
Sparse Core Ops, SparseCore 0:
  8.9 84.7 all-gather.1
  108.5 237.7 all-reduce.2
where the time goes:
time: 517 us; the launch traced here: 507 us
  waiting for transfers between devices  285 us (55%)
  matrix products  134 us (26%)
  other arithmetic  53.1 us (10%)
  between operations  34 us (7%)
    psum x1, waiting for transfers between devices, shards(): panels, factor_pivots = lax.psum((panel_local, factor_local), 'col')  238 us
    dot_general x1, matrix products, shards(): jnp.dot(stacked, factor_all.astype(jnp.float32), precision=lax.Precision....  60.7 us
    dot_general x7, matrix products, shards(): jnp.dot(stacked, factor_slice, precision=lax.Precision.HIGHEST)  57.1 us
    all_gather x1, waiting for transfers between devices, shards(): factor_all = lax.all_gather(factor_rows, 'row', axis=0, tiled=True)  46.3 us
    unnamed x15, other arithmetic  28.6 us
    dynamic_update_slice x8, other arithmetic, shards(): lax.dynamic_update_slice_in_dim(current, new_slice, start_list[step], 1)  20.3 us
    dot_general x8, matrix products, shards(): jnp.dot(panel_now, diag_inverse[step].astype(jnp.float32), precision=lax....  15.8 us
  transfers between devices with their start and end apart: 2, of which 2 were waited for; matrix products, arithmetic and copies ran while one was open for 4% of the time, Pallas kernels for 0%

commit v1 on v0

v1 whole, which is shorter than its diff:
```python
import functools

import jax
import jax.numpy as jnp
from jax import lax
from jax.experimental import pallas as pl
from jax.experimental.pallas import tpu as pltpu
from jax.sharding import PartitionSpec as P


F32 = jnp.float32
BF16 = jnp.bfloat16
TOP = 32767.0
TAIL = 16
TILE = 256


def eye_of(n):
    return lax.broadcasted_iota(jnp.int32, (n, n), 0) == lax.broadcasted_iota(jnp.int32, (n, n), 1)


def pack_kernel(block, half, idx_ref, w_ref, a_ref, b_ref):
    for part, out in enumerate((a_ref, b_ref)):
        x = w_ref[part * half : (part + 1) * half, :]
        top = jnp.maximum(jnp.max(jnp.abs(x), axis=1, keepdims=True), 1e-30)
        level = jnp.ceil(jnp.log2(top))
        coded = jnp.clip(jnp.round(x * (TOP * jnp.exp2(-level))), -TOP, TOP)
        out[0, :half, :] = coded.astype(jnp.int32).astype(jnp.int16)
        tail = jnp.zeros((TAIL, block), F32)
        row = lax.broadcasted_iota(jnp.int32, (TAIL, block), 0)
        for t in range(half // block):
            spread = jnp.where(eye_of(block), level[t * block : (t + 1) * block], 0.0)
            line = jnp.sum(spread, axis=0, keepdims=True)
            tail = jnp.where(row == t, line, tail)
        out[0, half:, :] = tail.astype(jnp.int32).astype(jnp.int16)


def pack(weights, index, count, block, part):
    rows = weights.shape[0] // 2
    half = rows // 2
    shape = jax.ShapeDtypeStruct((count, half + TAIL, block), jnp.int16)
    return pl.pallas_call(
        functools.partial(pack_kernel, block, half),
        grid_spec=pltpu.PrefetchScalarGridSpec(
            num_scalar_prefetch=1,
            grid=(count,),
            in_specs=[pl.BlockSpec((rows, block), lambda m, idx: (part, idx[m]))],
            out_specs=[pl.BlockSpec((1, half + TAIL, block), lambda m, idx: (m, 0, 0))] * 2,
        ),
        out_shape=[shape, shape],
        name="pack",
    )(index, weights)


def gather_rows(chip, core, chips, shard, pieces, span, target, sems):
    own, sown, far, sfar = pieces
    todo = [(own.at[:, span], chip * 2 + core), (sown.at[:, span], chip * 2 + 1 - core)]
    for q in range(chips - 1):
        there = lax.rem(chip - q - 1 + chips, chips)
        todo.append((far.at[pl.ds(q * shard, shard), :], there * 2 + core))
        todo.append((sfar.at[pl.ds(q * shard, shard), :], there * 2 + 1 - core))
    return [
        pltpu.make_async_copy(
            src, target.at[pl.ds(pl.multiple_of(at * shard, shard), shard), :], sems.at[n]
        )
        for n, (src, at) in enumerate(todo)
    ]


def chain_kernel(geo, *refs):
    groups, n_rel, count, pivots, block, tile, half, shard, base = geo
    rel_ref, rank_ref, tiles_ref, where_ref = refs[:4]
    n_src = groups * 2 * n_rel
    sources = refs[4 : 4 + n_src]
    f_pieces = refs[4 + n_src : 8 + n_src]
    d_ref, hi_ref, lo_ref, coded, tails, cur, f_all, sems, f_sems = refs[8 + n_src :]
    step = pl.program_id(0)
    per_half = half // tile
    sub = tile // block
    depth = pivots * block
    chips = depth // shard // 2
    first = pl.multiple_of(lax.rem(step, per_half) * tile, tile)

    def f_copies():
        return gather_rows(
            where_ref[0], where_ref[1], chips, shard, f_pieces, pl.ds(0, depth), f_all, f_sems
        )

    @pl.when(step == 0)
    def _():
        for copy in f_copies():
            copy.start()

    def copies(k, ref):
        rank = lax.rem(rank_ref[k], count)
        return (
            pltpu.make_async_copy(ref.at[rank, pl.ds(first, tile), :], coded.at[k], sems.at[0, k]),
            pltpu.make_async_copy(ref.at[rank, pl.ds(half, TAIL), :], tails.at[k], sems.at[1, k]),
        )

    @pl.loop(0, pivots)
    def _(k):
        for group in range(groups):
            for part in range(2):
                for rel in range(n_rel):
                    ref = sources[(group * 2 + part) * n_rel + rel]
                    here = (step // per_half == part) & (rel_ref[k] == rel)

                    @pl.when(here & (rank_ref[k] // count == group))
                    def _(ref=ref):
                        for copy in copies(k, ref):
                            copy.start()

    eye = eye_of(block)
    row = lax.broadcasted_iota(jnp.int32, (TAIL, block), 0)
    for k in range(pivots):
        for copy in copies(k, sources[0]):
            copy.wait()
        tail = tails[k].astype(jnp.int32).astype(F32)
        for t in range(sub):
            here = lax.rem(step, per_half) * sub + t
            line = jnp.sum(jnp.where(row == here, tail, 0.0), axis=0, keepdims=True)
            level = jnp.sum(jnp.where(eye, line, 0.0), axis=1, keepdims=True)
            span = slice(t * block, (t + 1) * block)
            value = coded[k, span, :].astype(jnp.int32).astype(F32)
            cur[span, k * block : (k + 1) * block] = value * (jnp.exp2(level) * (1.0 / TOP))

    @pl.when(step == 0)
    def _():
        for copy in f_copies():
            copy.wait()

    for k in range(pivots):
        cols = slice(k * block, (k + 1) * block)
        now = cur[:, cols]
        now_hi = now.astype(BF16)
        now_lo = (now - now_hi.astype(F32)).astype(BF16)
        diag = d_ref[k]
        err = jnp.dot(
            jnp.concatenate([now_hi, now_lo], axis=1),
            jnp.concatenate([diag, diag], axis=0),
            preferred_element_type=F32,
        )
        parts = []
        for t in range(sub):
            flag = tiles_ref[base + step * sub + t, k].astype(F32)
            parts.append(err[t * block : (t + 1) * block] * flag)
        err = jnp.concatenate(parts, axis=0)
        hi = err.astype(BF16)
        lo = (err - hi.astype(F32)).astype(BF16)
        hi_ref[:, cols] = hi
        lo_ref[:, cols] = lo
        if k + 1 < pivots:
            f = f_all[cols, (k + 1) * block :]
            both = jnp.concatenate([hi, lo], axis=1)
            cur[:, (k + 1) * block :] -= jnp.dot(
                both, jnp.concatenate([f, f], axis=0), preferred_element_type=F32
            )


def chain(count, rel, rank, tiles, where, sources, f_pieces, diag, rows, shard, part):
    pivots, block, _ = diag.shape
    half = rows // 2
    tile = min(512, half)
    groups = len(sources)
    n_rel = len(sources[0]) // 2
    flat = [x for group in sources for x in group]
    depth = pivots * block
    shape = jax.ShapeDtypeStruct((rows, depth), BF16)
    anywhere = pl.BlockSpec(memory_space=pl.ANY)
    geo = (groups, n_rel, count, pivots, block, tile, half, shard, part * rows // block)
    return pl.pallas_call(
        functools.partial(chain_kernel, geo),
        grid_spec=pltpu.PrefetchScalarGridSpec(
            num_scalar_prefetch=4,
            grid=(rows // tile,),
            in_specs=[anywhere] * (len(flat) + 4)
            + [pl.BlockSpec(diag.shape, lambda i, *_: (0, 0, 0))],
            out_specs=[pl.BlockSpec((tile, depth), lambda i, *_: (i, 0))] * 2,
            scratch_shapes=[
                pltpu.VMEM((pivots, tile, block), jnp.int16),
                pltpu.VMEM((pivots, TAIL, block), jnp.int16),
                pltpu.VMEM((tile, depth), F32),
                pltpu.VMEM((depth, depth), BF16),
                pltpu.SemaphoreType.DMA((2, pivots)),
                pltpu.SemaphoreType.DMA((depth // shard,)),
            ],
        ),
        out_shape=[shape, shape],
        cost_estimate=pl.CostEstimate(
            flops=4 * rows * depth * depth, bytes_accessed=8 * rows * depth, transcendentals=0
        ),
        name="chain",
    )(rel, rank, tiles, where, *flat, *f_pieces, diag)


def pick_kernel(local_ref, mine_ref, f_ref, o_ref):
    k = pl.program_id(0)
    o_ref[...] = (f_ref[...].astype(F32) * mine_ref[k].astype(F32)).astype(BF16)


def pick(factor_rows, local, mine, block):
    shard = factor_rows.shape[0]
    pivots = local.shape[0]
    return pl.pallas_call(
        pick_kernel,
        grid_spec=pltpu.PrefetchScalarGridSpec(
            num_scalar_prefetch=2,
            grid=(pivots,),
            in_specs=[pl.BlockSpec((shard, block), lambda k, local, mine: (0, local[k]))],
            out_specs=pl.BlockSpec((shard, block), lambda k, *_: (0, k)),
        ),
        out_shape=jax.ShapeDtypeStruct((shard, pivots * block), BF16),
        name="pick",
    )(local, mine, factor_rows)


def main_kernel(geo, where_ref, kind_ref, tiles_ref, hi_ref, lo_ref, w_ref, *refs):
    block, pivots, shard, chips, width, tile, offset, base = geo
    own, sown, far, sfar = refs[:4]
    o_ref, f, sems = refs[-3:]
    step = pl.program_id(0)
    chip = where_ref[0]
    core = where_ref[1]

    def pieces():
        return gather_rows(chip, core, chips, shard, (own, sown, far, sfar), pl.ds(offset, width), f, sems)

    @pl.when(step == 0)
    def _():
        for copy in pieces():
            copy.start()
        for copy in pieces():
            copy.wait()
        row = lax.broadcasted_iota(jnp.int32, (pivots * block, block), 0)
        for b in range(width // block):
            kind = kind_ref[offset // block + b]

            @pl.when(kind < pivots)
            def _(b=b, kind=kind):
                cols = slice(b * block, (b + 1) * block)
                f[:, cols] = jnp.where(row < kind * block, f[:, cols].astype(F32), 0.0).astype(BF16)

    acc = jnp.dot(hi_ref[...], f[...], preferred_element_type=F32)
    acc += jnp.dot(lo_ref[...], f[...], preferred_element_type=F32)
    o_ref[...] = w_ref[...] - acc
    for b in range(width // block):
        kind = kind_ref[offset // block + b]

        @pl.when(kind < pivots)
        def _(b=b, kind=kind):
            for t in range(tile // block):
                flag = 1 - tiles_ref[(base + step) * (tile // block) + t, kind]
                at = (slice(t * block, (t + 1) * block), slice(b * block, (b + 1) * block))
                o_ref[at] = o_ref[at] * flag.astype(F32)


def main_step(where, kind, tiles, hi, lo, weights, pieces, out, offset, width, shard, block, pivots, part):
    rows, depth = hi.shape
    tile = min(TILE, rows)
    base = part * rows // tile
    chips = depth // shard // 2
    chunk = offset // width
    geo = (block, pivots, shard, chips, width, tile, offset, base)
    anywhere = pl.BlockSpec(memory_space=pl.ANY)
    in_specs = [
        pl.BlockSpec((tile, depth), lambda i, *_: (i, 0)),
        pl.BlockSpec((tile, depth), lambda i, *_: (i, 0)),
        pl.BlockSpec((tile, width), lambda i, *_: (base + i, chunk)),
    ] + [anywhere] * 4
    args = [where, kind, tiles, hi, lo, weights, *pieces]
    aliases = {}
    if out is not None:
        in_specs.append(anywhere)
        args.append(out)
        aliases = {len(args) - 1: 0}
    return pl.pallas_call(
        functools.partial(main_kernel, geo),
        grid_spec=pltpu.PrefetchScalarGridSpec(
            num_scalar_prefetch=3,
            grid=(rows // tile,),
            in_specs=in_specs,
            out_specs=pl.BlockSpec((tile, width), lambda i, *_: (base + i, chunk)),
            scratch_shapes=[
                pltpu.VMEM((depth, width), BF16),
                pltpu.SemaphoreType.DMA((2 * chips,)),
            ],
        ),
        out_shape=jax.ShapeDtypeStruct(weights.shape, F32),
        input_output_aliases=aliases,
        cost_estimate=pl.CostEstimate(
            flops=4 * rows * depth * width, bytes_accessed=8 * rows * width, transcendentals=0
        ),
        name="main",
    )(*args)


def program(n_col, n_row, weights, factor_rows, diag_inverse, prune_tiles, pivot_order):
    rows, cols = weights.shape
    pivots, block, _ = diag_inverse.shape
    shard = factor_rows.shape[0]
    blocks_dev = cols // block
    wide = n_col // 2
    chips = n_row // 2
    me_col = lax.axis_index("col")
    me_row = lax.axis_index("row")
    chip = me_row // 2

    def up(x, r):
        pairs = [(z * 2 + c, z * 2 + 2 + c) for z in range(r, chips - 1) for c in range(2)]
        return lax.ppermute(x, "row", pairs)

    def down(x, r):
        pairs = [(z * 2 + c, z * 2 - 2 + c) for z in range(1, chips - r) for c in range(2)]
        return lax.ppermute(x, "row", pairs)

    def sibling(x):
        return lax.ppermute(x, "row", [(i, i ^ 1) for i in range(n_row)])

    def gather(x, own_sibling):
        ups, downs = [x], [x]
        for r in range(chips - 1):
            ups.append(up(ups[-1], r))
            downs.append(down(downs[-1], r))
        parts = [
            jnp.where(chip >= q + 1, ups[q + 1], downs[chips - 1 - q]) for q in range(chips - 1)
        ]
        joined = jnp.concatenate(parts, axis=0)
        return own_sibling, joined, sibling(joined)

    def swap_lo(x):
        return lax.ppermute(x, "col", [(i, i ^ 1) for i in range(n_col)])

    def shift_hi(x, d):
        pairs = [(((h + d) % wide) * 2 + l, h * 2 + l) for h in range(wide) for l in range(2)]
        return lax.ppermute(x, "col", pairs)

    owner = pivot_order // blocks_dev
    local = pivot_order % blocks_dev
    ks = jnp.arange(pivots, dtype=jnp.int32)
    same = owner[:, None] == owner[None, :]
    rank = jnp.sum((same & (ks[None, :] < ks[:, None])).astype(jnp.int32), axis=1)
    mine = owner == me_col
    place = (rank[None, :] == ks[:, None]) & mine[None, :]
    index = jnp.sum(jnp.where(place, local[None, :], 0), axis=1)
    rel_hi = (owner // 2 - me_col // 2 + wide) % wide
    rel = rel_hi * 2 + (owner % 2 != me_col % 2).astype(jnp.int32)
    block_ids = jnp.arange(blocks_dev, dtype=jnp.int32)
    hit = (block_ids[:, None] == local[None, :]) & mine[None, :]
    kind = jnp.min(jnp.where(hit, ks[None, :], pivots), axis=1)
    where = jnp.stack([chip, me_row % 2]).astype(jnp.int32)

    f_pick = pick(factor_rows, local, mine.astype(jnp.int32), block)
    f_pick = f_pick + swap_lo(f_pick)
    f_here = f_pick
    for d in range(1, wide):
        f_here = f_here + shift_hi(f_pick, d)
    f_pieces = (f_here,) + gather(f_here, sibling(f_here))

    def exchange(index, count, part):
        a, b = pack(weights, index, count, block, part)
        far = range(1, wide)
        a_lo = swap_lo(a)
        b_hi = [shift_hi(b, d) for d in far]
        b_lo = swap_lo(b)
        a_hi = [shift_hi(a, d) for d in far]
        a_far = [shift_hi(a_lo, d) for d in far]
        b_far = [swap_lo(x) for x in b_hi]
        a_all = [a, a_lo]
        b_all = [b, b_lo]
        for d in range(wide - 1):
            a_all += [a_hi[d], a_far[d]]
            b_all += [b_hi[d], b_far[d]]
        return a_all + b_all

    count = (pivots + 1) // 2
    crowded = jnp.max(rank) >= count
    errors = []
    for part in range(2):
        near = exchange(index[:count], count, part)

        def run(sources, part=part):
            return chain(
                count, rel, rank, prune_tiles, where, sources, f_pieces, diag_inverse,
                rows // 2, shard, part,
            )

        def few(near=near, run=run):
            return run([near])

        def many(near=near, run=run, part=part):
            return run([near, exchange(index[count:], count, part)])

        errors.append(lax.cond(crowded, many, few))

    widths = [cols // 2, cols // 2]
    sown = sibling(factor_rows)
    out = None
    offset = 0
    for width in widths:
        far = gather(factor_rows[:, offset : offset + width], sown)
        for part in range(2):
            hi, lo = errors[part]
            out = main_step(
                where, kind, prune_tiles, hi, lo, weights, (factor_rows,) + far, out, offset,
                width, shard, block, pivots, part,
            )
        offset += width
    return out


def solution(mesh):
    n_col, n_row = mesh.shape["col"], mesh.shape["row"]
    return jax.shard_map(
        functools.partial(program, n_col, n_row),
        mesh=mesh,
        in_specs=(P("row", "col"), P("row", "col"), P(), P("row", None), P()),
        out_specs=P("row", "col"),
        check_vma=False,
    )
```

time: 517 us -> 293 us (0.57); the launches traced: 507 us -> 292 us
  waiting for transfers between devices: 285 us -> 113 us
  matrix products: 134 us -> 0 us
  Pallas kernels: 0 us -> 106 us
  starting transfers between devices: 0.04 us -> 50.4 us
  other arithmetic: 53.1 us -> 11.8 us
  between operations: 34 us -> 1.27 us
  local copies, waits for them, and re-layouts: 1.81 us -> 9.48 us
    psum x1 -> x0, waiting for transfers between devices: 238 us -> none  [shards(): panels, factor_pivots = lax.psum((panel_local, factor_local), 'col')]
    dot_general x16 -> x0, matrix products: 134 us -> none  [the longest x1 60.7 us: shards(): jnp.dot(stacked, factor_all.astype(jnp.float32), precision=lax.Precision....]
    ppermute x0 -> x37, waiting for transfers between devices: none -> 113 us  [the longest x9 57.2 us: down(): return lax.ppermute(x, 'row', pairs)]
    pallas_call x0 -> x9, Pallas kernels: none -> 106 us  [the longest x4 67.6 us: main_step(): pl.pallas_call(functools.partial(main_kernel, geo), grid_spec=pltpu.Prefe...]
    ppermute x0 -> x37, starting transfers between devices: none -> 50.4 us  [the longest x9 19.9 us: up(): return lax.ppermute(x, 'row', pairs)]
    all_gather x1 -> x0, waiting for transfers between devices: 46.3 us -> none  [shards(): factor_all = lax.all_gather(factor_rows, 'row', axis=0, tiled=True)]
    unnamed x15 -> x0, other arithmetic: 28.6 us -> none
    dynamic_update_slice x8 -> x0, other arithmetic: 20.3 us -> none  [shards(): lax.dynamic_update_slice_in_dim(current, new_slice, start_list[step], 1)]
  transfers between devices with their start and end apart: 2 -> 37, of which waited for: 2 -> 16; matrix products, arithmetic and copies ran while one was open for 4% -> 4% of each run, Pallas kernels for 0% -> 23%
where the time goes in v1:
time: 293 us; the launch traced here: 292 us
  waiting for transfers between devices  113 us (39%)
  Pallas kernels  106 us (36%)
  starting transfers between devices  50.4 us (17%)
  other arithmetic  11.8 us (4%)
  local copies, waits for them, and re-layouts  9.48 us (3%)
    pallas_call x4, Pallas kernels, main_step(): pl.pallas_call(functools.partial(main_kernel, geo), grid_spec=pltpu.Prefe...  67.6 us
    ppermute x9, waiting for transfers between devices, down(): return lax.ppermute(x, 'row', pairs)  57.2 us
    ppermute x7, waiting for transfers between devices, shift_hi(): return lax.ppermute(x, 'col', pairs)  41.9 us
    pallas_call x2, Pallas kernels, chain(): pl.pallas_call(functools.partial(chain_kernel, geo), grid_spec=pltpu.Pref...  24.3 us
    ppermute x9, starting transfers between devices, up(): return lax.ppermute(x, 'row', pairs)  19.9 us
    ppermute x9, starting transfers between devices, down(): return lax.ppermute(x, 'row', pairs)  11.8 us
    ppermute x7, waiting for transfers between devices, swap_lo(): return lax.ppermute(x, 'col', [(i, i ^ 1) for i in range(n_col)])  11.3 us
    ppermute x7, starting transfers between devices, swap_lo(): return lax.ppermute(x, 'col', [(i, i ^ 1) for i in range(n_col)])  9.42 us
  transfers between devices with their start and end apart: 37, of which 16 were waited for; matrix products, arithmetic and copies ran while one was open for 4% of the time, Pallas kernels for 23%

profile of v1, /device:TPU:0, one launch (start us, length us, event | category | flops | bytes accessed | tf_op | source)
XLA Modules:
  0.0 291.6 jit_solution(12380262158054935274)
XLA Ops:
  2.4 5.0 %pick.1 = bf16[128,1024]{1,0:T(8,128)(2,1)} custom-call(s32[8]{0:T(128)} %and_select_fusion.4.local_ref, s32[8]{0:T(128)} %get-tuple-element.385.mine_ref, bf16[128,4096]{1,0:T(8,128)(2,1)} %refs_0_.7), custom_call_target="tpu_custom_call" | custom-call | tf_op jit(solution)/shard_map/pick/pallas_call | solution.py:205
  7.5 3.0 %collective-permute-start.18 = (bf16[128,1024]{1,0:T(8,128)(2,1)}, bf16[128,1024]{1,0:T(8,128)(2,1)S(1)}, u32[]{:S(2)}, u32[]{:S(2)}) collective-permute-start(bf16[128,1024]{1,0:T(8,128)(2,1)} %pick.1), channel_id=1, source_target_pairs={{0,8},{8,0},{16,24},{24,16},{1,9},{9,1},{17,25},{25,17},{2,10},{10... | collective-permute-start | bytes 786440 | tf_op jit(solution)/shard_map/ppermute | solution.py:332
  10.4 6.5 %collective-permute-done.18 = bf16[128,1024]{1,0:T(8,128)(2,1)S(1)} collective-permute-done((bf16[128,1024]{1,0:T(8,128)(2,1)}, bf16[128,1024]{1,0:T(8,128)(2,1)S(1)}, u32[]{:S(2)}, u32[]{:S(2)}) %collective-permute-start.18) | collective-permute-done | bytes 262176 | tf_op jit(solution)/shard_map/ppermute | solution.py:332
  18.0 1.8 collective-permute-start.19
  19.8 5.7 %collective-permute-done.19 = bf16[128,1024]{1,0:T(8,128)(2,1)S(1)} collective-permute-done((bf16[128,1024]{1,0:T(8,128)(2,1)S(1)}, bf16[128,1024]{1,0:T(8,128)(2,1)S(1)}, u32[]{:S(2)}, u32[]{:S(2)}) %collective-permute-start.19) | collective-permute-done | bytes 262176 | tf_op jit(solution)/shard_map/ppermute | solution.py:336
  25.6 3.5 %collective-permute-start.21 = (bf16[128,1024]{1,0:T(8,128)(2,1)S(1)}, bf16[128,1024]{1,0:T(8,128)(2,1)S(1)}, u32[]{:S(2)}, u32[]{:S(2)}) collective-permute-start(bf16[128,1024]{1,0:T(8,128)(2,1)S(1)} %add.45), channel_id=1, source_target_pairs={{0,2},{1,3},{2,4},{3,5},{4,6},{5,7},{8,10},{9,11},{10,12},{11,13},... | collective-permute-start | bytes 786440 | tf_op jit(solution)/shard_map/ppermute | solution.py:311
  29.0 1.3 collective-permute-start.22
  30.3 2.6 collective-permute-done.21
  33.6 3.7 %collective-permute-done.22 = bf16[128,1024]{1,0:T(8,128)(2,1)S(1)} collective-permute-done((bf16[128,1024]{1,0:T(8,128)(2,1)S(1)}, bf16[128,1024]{1,0:T(8,128)(2,1)S(1)}, u32[]{:S(2)}, u32[]{:S(2)}) %collective-permute-start.22) | collective-permute-done | bytes 262176 | tf_op jit(solution)/shard_map/ppermute | solution.py:315
  37.3 1.3 collective-permute-start.23
  39.6 4.4 %pack.7 = (s16[4,528,128]{2,1,0:T(8,128)(2,1)}, s16[4,528,128]{2,1,0:T(8,128)(2,1)}) custom-call(s32[4]{0:T(128)S(1)} %bitcast.3, f32[2048,4096]{1,0:T(8,128)} %w_ref.11), custom_call_target="tpu_custom_call" | custom-call | tf_op jit(solution)/shard_map/pack/pallas_call | solution.py:42
  45.1 2.0 collective-permute-start.37
  47.1 1.3 collective-permute-start.24
  48.5 8.2 %collective-permute-done.24 = bf16[128,1024]{1,0:T(8,128)(2,1)S(1)} collective-permute-done((bf16[128,1024]{1,0:T(8,128)(2,1)S(1)}, bf16[128,1024]{1,0:T(8,128)(2,1)S(1)}, u32[]{:S(2)}, u32[]{:S(2)}) %collective-permute-start.24) | collective-permute-done | bytes 262176 | tf_op jit(solution)/shard_map/ppermute | solution.py:315
  57.9 1.8 collective-permute-start.38
  59.7 12.4 %collective-permute-done.40 = s16[4,528,128]{2,1,0:T(8,128)(2,1)} collective-permute-done((s16[4,528,128]{2,1,0:T(8,128)(2,1)}, s16[4,528,128]{2,1,0:T(8,128)(2,1)}, u32[]{:S(2)}, u32[]{:S(2)}) %collective-permute-start.40) | collective-permute-done | bytes 540704 | tf_op jit(solution)/shard_map/ppermute | solution.py:336
  73.2 4.4 %pack.6 = (s16[4,528,128]{2,1,0:T(8,128)(2,1)}, s16[4,528,128]{2,1,0:T(8,128)(2,1)}) custom-call(s32[4]{0:T(128)S(1)} %bitcast.4, f32[2048,4096]{1,0:T(8,128)} %w_ref.11), custom_call_target="tpu_custom_call" | custom-call | tf_op jit(solution)/shard_map/pack/pallas_call | solution.py:42
  79.6 4.8 %collective-permute-done.41 = s16[4,528,128]{2,1,0:T(8,128)(2,1)} collective-permute-done((s16[4,528,128]{2,1,0:T(8,128)(2,1)}, s16[4,528,128]{2,1,0:T(8,128)(2,1)}, u32[]{:S(2)}, u32[]{:S(2)}) %collective-permute-start.41) | collective-permute-done | bytes 540704 | tf_op jit(solution)/shard_map/ppermute | solution.py:332
  85.3 12.8 %conditional.3 = ((bf16[1024,1024]{1,0:T(8,128)(2,1)}, bf16[1024,1024]{1,0:T(8,128)(2,1)})) conditional(s32[]{:T(128)} %convert_element_type.14, (s32[8]{0:T(128)S(1)}, s32[8]{0:T(128)S(1)}, s32[16,8]{0,1:T(8,128)S(1)}, s32[2]{0:T(128)S(1)}, s16[4,528,128]{2,1,0:T(8,128)(2,1)}, /*index=5*/s16[4,528,128]{2,1,0:T(8,128)(2,1)}, ...), branch_computations={%region_6.7_spmd, %region_7.8_spmd} | conditional | flops 4294967296 | bytes 21366040 | solution.py:394
  85.9 12.2 %chain.6 = (bf16[1024,1024]{1,0:T(8,128)(2,1)}, bf16[1024,1024]{1,0:T(8,128)(2,1)}) custom-call(s32[8]{0:T(128)S(1)} %get-tuple-element.187.refs_0_, s32[8]{0:T(128)S(1)} %get-tuple-element.188.refs_1_, s32[16,8]{1,0:T(8,128)} %copy.19.refs_2_, s32[2]{0:T(128)S(1)} %get-tuple-element.190.refs_3_, s16[4,528,128]{2,1,0:T(8,128)(2,1)} %get-tuple-element.191.refs_4_, ...), custom_call_target="tpu_custom_call" | custom-call | flops 4294967296 | bytes 8388608 | tf_op jit(solution)/shard_map/cond/branch_0_fun/chain/pallas_call | solution.py:172
  98.1 1.9 collective-permute-start.16
  100.2 1.4 collective-permute-start.15
  102.8 10.7 %collective-permute-done.16 = s16[4,528,128]{2,1,0:T(8,128)(2,1)S(1)} collective-permute-done((s16[4,528,128]{2,1,0:T(8,128)(2,1)}, s16[4,528,128]{2,1,0:T(8,128)(2,1)S(1)}, u32[]{:S(2)}, u32[]{:S(2)}) %collective-permute-start.16) | collective-permute-done | bytes 540704 | tf_op jit(solution)/shard_map/ppermute | solution.py:336
  113.5 1.4 collective-permute-start.17
  116.0 2.9 collective-permute-start.42
  118.9 6.2 %collective-permute-done.13 = s16[4,528,128]{2,1,0:T(8,128)(2,1)S(1)} collective-permute-done((s16[4,528,128]{2,1,0:T(8,128)(2,1)}, s16[4,528,128]{2,1,0:T(8,128)(2,1)S(1)}, u32[]{:S(2)}, u32[]{:S(2)}) %collective-permute-start.13) | collective-permute-done | bytes 540704 | tf_op jit(solution)/shard_map/ppermute | solution.py:336
  125.1 6.8 %collective-permute-done.14 = s16[4,528,128]{2,1,0:T(8,128)(2,1)S(1)} collective-permute-done((s16[4,528,128]{2,1,0:T(8,128)(2,1)}, s16[4,528,128]{2,1,0:T(8,128)(2,1)S(1)}, u32[]{:S(2)}, u32[]{:S(2)}) %collective-permute-start.14) | collective-permute-done | bytes 540704 | tf_op jit(solution)/shard_map/ppermute | solution.py:336
  131.9 16.8 %conditional.2 = ((bf16[1024,1024]{1,0:T(8,128)(2,1)}, bf16[1024,1024]{1,0:T(8,128)(2,1)})) conditional(s32[]{:T(128)} %convert_element_type.14, (s32[8]{0:T(128)S(1)}, s32[8]{0:T(128)S(1)}, s32[16,8]{0,1:T(8,128)S(1)}, s32[2]{0:T(128)S(1)}, s16[4,528,128]{2,1,0:T(8,128)(2,1)}, /*index=5*/s16[4,528,128]{2,1,0:T(8,128)(2,1)}, ...), branch_computations={%region_4.5_spmd, %region_5.6_spmd} | conditional | flops 4294967296 | bytes 32179620 | solution.py:394
  136.6 12.1 %chain.4 = (bf16[1024,1024]{1,0:T(8,128)(2,1)}, bf16[1024,1024]{1,0:T(8,128)(2,1)}) custom-call(s32[8]{0:T(128)S(1)} %get-tuple-element.149.refs_0_, s32[8]{0:T(128)S(1)} %get-tuple-element.150.refs_1_, s32[16,8]{1,0:T(8,128)} %copy.17.refs_2_, s32[2]{0:T(128)S(1)} %get-tuple-element.152.refs_3_, s16[4,528,128]{2,1,0:T(8,128)(2,1)} %get-tuple-element.153.refs_4_, ...), custom_call_target="tpu_custom_call" | custom-call | flops 4294967296 | bytes 8388608 | tf_op jit(solution)/shard_map/cond/branch_0_fun/chain/pallas_call | solution.py:172
  148.8 1.3 collective-permute-start.43
  150.1 1.3 collective-permute-start.30
  151.4 7.1 %collective-permute-start.29 = (bf16[128,2048]{1,0:T(8,128)(2,1)}, bf16[128,2048]{1,0:T(8,128)(2,1)S(1)}, u32[]{:S(2)}, u32[]{:S(2)}) collective-permute-start(bf16[128,2048]{1,0:T(8,128)(2,1)} %get-tuple-element.389), channel_id=1, source_target_pairs={{0,2},{1,3},{2,4},{3,5},{4,6},{5,7},{8,10},{9,11},{10,12},{11,13},... | collective-permute-start | bytes 1572872 | tf_op jit(solution)/shard_map/ppermute | solution.py:311
  158.5 1.5 collective-permute-start.46
  160.0 7.7 %collective-permute-done.43 = bf16[128,2048]{1,0:T(8,128)(2,1)} collective-permute-done((bf16[128,2048]{1,0:T(8,128)(2,1)}, bf16[128,2048]{1,0:T(8,128)(2,1)}, u32[]{:S(2)}, u32[]{:S(2)}) %collective-permute-start.43) | collective-permute-done | bytes 524320 | tf_op jit(solution)/shard_map/ppermute | solution.py:315
  167.7 1.3 collective-permute-start.44
  169.0 9.9 %collective-permute-done.30 = bf16[128,2048]{1,0:T(8,128)(2,1)} collective-permute-done((bf16[128,2048]{1,0:T(8,128)(2,1)}, bf16[128,2048]{1,0:T(8,128)(2,1)}, u32[]{:S(2)}, u32[]{:S(2)}) %collective-permute-start.30) | collective-permute-done | bytes 524320 | tf_op jit(solution)/shard_map/ppermute | solution.py:315
  180.2 1.4 collective-permute-start.33
  181.7 1.5 collective-permute-start.47
  184.5 5.7 %collective-permute-done.44 = bf16[128,2048]{1,0:T(8,128)(2,1)} collective-permute-done((bf16[128,2048]{1,0:T(8,128)(2,1)}, bf16[128,2048]{1,0:T(8,128)(2,1)}, u32[]{:S(2)}, u32[]{:S(2)}) %collective-permute-start.44) | collective-permute-done | bytes 524320 | tf_op jit(solution)/shard_map/ppermute | solution.py:315
  193.3 8.1 %collective-permute-done.31 = bf16[128,2048]{1,0:T(8,128)(2,1)} collective-permute-done((bf16[128,2048]{1,0:T(8,128)(2,1)}, bf16[128,2048]{1,0:T(8,128)(2,1)}, u32[]{:S(2)}, u32[]{:S(2)}) %collective-permute-start.31) | collective-permute-done | bytes 524320 | tf_op jit(solution)/shard_map/ppermute | solution.py:315
  201.4 1.5 collective-permute-start.32
  204.0 8.5 %collective-permute-done.45 = bf16[128,2048]{1,0:T(8,128)(2,1)S(1)} collective-permute-done((bf16[128,2048]{1,0:T(8,128)(2,1)}, bf16[128,2048]{1,0:T(8,128)(2,1)S(1)}, u32[]{:S(2)}, u32[]{:S(2)}) %collective-permute-start.45) | collective-permute-done | bytes 524320 | tf_op jit(solution)/shard_map/ppermute | solution.py:315
  212.8 1.5 broadcast_select_fusion.3
  215.5 5.5 %collective-permute-done.32 = bf16[128,2048]{1,0:T(8,128)(2,1)S(1)} collective-permute-done((bf16[128,2048]{1,0:T(8,128)(2,1)}, bf16[128,2048]{1,0:T(8,128)(2,1)S(1)}, u32[]{:S(2)}, u32[]{:S(2)}) %collective-permute-start.32) | collective-permute-done | bytes 524320 | tf_op jit(solution)/shard_map/ppermute | solution.py:315
  223.8 16.9 %main.4.refs_4_ = f32[2048,4096]{1,0:T(8,128)} custom-call(s32[2]{0:T(128)S(1)} %pad_add_fusion.where_ref, s32[32]{0:T(128)} %select_reduce_fusion.1.kind_ref, s32[16,8]{1,0:T(8,128)} %copy.24.tiles_ref, bf16[1024,1024]{1,0:T(8,128)(2,1)} %get-tuple-element.239.hi_ref, bf16[1024,1024]{1,0:T(8,128)(2,1)} %get-tuple-element.240.lo_ref, f32[2048,4096]{1,0:T(8,128)} %w_ref.11, ...), custom_call_target="tpu_custom_call" | custom-call | flops 8589934592 | bytes 16777216 | tf_op jit(solution)/shard_map/main/pallas_call | solution.py:277
  240.7 17.0 %main.5.refs_4_ = f32[2048,4096]{1,0:T(8,128)} custom-call(s32[2]{0:T(128)S(1)} %pad_add_fusion.where_ref, s32[32]{0:T(128)} %select_reduce_fusion.1.kind_ref, s32[16,8]{1,0:T(8,128)} %copy.24.tiles_ref, bf16[1024,1024]{1,0:T(8,128)(2,1)} %get-tuple-element.235.hi_ref, ...), custom_call_target="tpu_custom_call", output_to_operand_aliasing={{}: (10, {})} | custom-call | flops 8589934592 | bytes 16777216 | tf_op jit(solution)/shard_map/main/pallas_call | solution.py:277
  257.7 16.5 %main.6.refs_4_ = f32[2048,4096]{1,0:T(8,128)} custom-call(s32[2]{0:T(128)S(1)} %pad_add_fusion.where_ref, s32[32]{0:T(128)} %select_reduce_fusion.1.kind_ref, s32[16,8]{1,0:T(8,128)} %copy.24.tiles_ref, bf16[1024,1024]{1,0:T(8,128)(2,1)S(1)} %copy-done.3, bf16[1024,1024]{1,0:T(8,128)(2,1)} %get-tuple-element.240.lo_ref, ...), custom_call_target="tpu_custom_call", output_to_operand_aliasing={{}: (10, {})} | custom-call | flops 8589934592 | bytes 16777216 | tf_op jit(solution)/shard_map/main/pallas_call | solution.py:277
  274.2 17.1 %main.7 = f32[2048,4096]{1,0:T(8,128)} custom-call(s32[2]{0:T(128)S(1)} %pad_add_fusion.where_ref, s32[32]{0:T(128)} %select_reduce_fusion.1.kind_ref, s32[16,8]{1,0:T(8,128)} %copy.24.tiles_ref, bf16[1024,1024]{1,0:T(8,128)(2,1)} %get-tuple-element.235.hi_ref, bf16[1024,1024]{1,0:T(8,128)(2,1)} %get-tuple-element.236.lo_ref, ...), custom_call_target="tpu_custom_call", output_to_operand_aliasing={{}: (10, {})} | custom-call | flops 8589934592 | bytes 16777216 | tf_op jit(solution)/shard_map/main/pallas_call | solution.py:277
  (91 shorter events, 29.8 us)
Async XLA Ops:
  1.2 38.3 %copy-start.6 = (s32[8]{0:T(128)S(1)}, s32[8]{0:T(128)}, u32[]{:S(2)}) copy-start(s32[8]{0:T(128)} %and_select_fusion.4.local_ref) | copy-start | bytes 100
  7.5 9.5 %collective-permute-start.18 = (bf16[128,1024]{1,0:T(8,128)(2,1)}, bf16[128,1024]{1,0:T(8,128)(2,1)S(1)}, u32[]{:S(2)}, u32[]{:S(2)}) collective-permute-start(bf16[128,1024]{1,0:T(8,128)(2,1)} %pick.1), channel_id=1, source_target_pairs={{0,8},{8,0},{16,24},{24,16},{1,9},{9,1},{17,25},{25,17},{2,10},{10... | collective-permute-start | bytes 786440 | tf_op jit(solution)/shard_map/ppermute | solution.py:332
  18.0 7.5 %collective-permute-start.19 = (bf16[128,1024]{1,0:T(8,128)(2,1)S(1)}, bf16[128,1024]{1,0:T(8,128)(2,1)S(1)}, u32[]{:S(2)}, u32[]{:S(2)}) collective-permute-start(bf16[128,1024]{1,0:T(8,128)(2,1)S(1)} %add.44), channel_id=1, source_target_pairs={{16,0},{24,8},{0,16},{8,24},{17,1},{25,9},{1,17},{9,25},{18,2},{26... | collective-permute-start | bytes 786440 | tf_op jit(solution)/shard_map/ppermute | solution.py:336
  25.6 7.3 %collective-permute-start.21 = (bf16[128,1024]{1,0:T(8,128)(2,1)S(1)}, bf16[128,1024]{1,0:T(8,128)(2,1)S(1)}, u32[]{:S(2)}, u32[]{:S(2)}) collective-permute-start(bf16[128,1024]{1,0:T(8,128)(2,1)S(1)} %add.45), channel_id=1, source_target_pairs={{0,2},{1,3},{2,4},{3,5},{4,6},{5,7},{8,10},{9,11},{10,12},{11,13},... | collective-permute-start | bytes 786440 | tf_op jit(solution)/shard_map/ppermute | solution.py:311
  29.0 8.3 %collective-permute-start.22 = (bf16[128,1024]{1,0:T(8,128)(2,1)S(1)}, bf16[128,1024]{1,0:T(8,128)(2,1)S(1)}, u32[]{:S(2)}, u32[]{:S(2)}) collective-permute-start(bf16[128,1024]{1,0:T(8,128)(2,1)S(1)} %add.45), channel_id=1, source_target_pairs={{2,0},{3,1},{4,2},{5,3},{6,4},{7,5},{10,8},{11,9},{12,10},{13,11},... | collective-permute-start | bytes 786440 | tf_op jit(solution)/shard_map/ppermute | solution.py:315
  32.9 5.9 %collective-permute-start.25 = (bf16[128,1024]{1,0:T(8,128)(2,1)S(1)}, bf16[128,1024]{1,0:T(8,128)(2,1)S(1)}, u32[]{:S(2)}, u32[]{:S(2)}) collective-permute-start(bf16[128,1024]{1,0:T(8,128)(2,1)S(1)} %collective-permute-done.21), channel_id=1, source_target_pairs={{2,4},{3,5},{4,6},{5,7},{10,12},{11,13},{12,14},{13,15},{18,20},{1... | collective-permute-start | bytes 786440 | tf_op jit(solution)/shard_map/ppermute | solution.py:311
  37.3 9.8 %collective-permute-start.23 = (bf16[128,1024]{1,0:T(8,128)(2,1)S(1)}, bf16[128,1024]{1,0:T(8,128)(2,1)S(1)}, u32[]{:S(2)}, u32[]{:S(2)}) collective-permute-start(bf16[128,1024]{1,0:T(8,128)(2,1)S(1)} %collective-permute-done.22), channel_id=1, source_target_pairs={{2,0},{3,1},{4,2},{5,3},{10,8},{11,9},{12,10},{13,11},{18,16},{19,... | collective-permute-start | bytes 786440 | tf_op jit(solution)/shard_map/ppermute | solution.py:315
  38.8 9.6 %collective-permute-start.26 = (bf16[128,1024]{1,0:T(8,128)(2,1)S(1)}, bf16[128,1024]{1,0:T(8,128)(2,1)S(1)}, u32[]{:S(2)}, u32[]{:S(2)}) collective-permute-start(bf16[128,1024]{1,0:T(8,128)(2,1)S(1)} %collective-permute-done.25), channel_id=1, source_target_pairs={{4,6},{5,7},{12,14},{13,15},{20,22},{21,23},{28,30},{29,31}} | collective-permute-start | bytes 786440 | tf_op jit(solution)/shard_map/ppermute | solution.py:311
  44.0 13.8 %collective-permute-start.36 = (s16[4,528,128]{2,1,0:T(8,128)(2,1)}, s16[4,528,128]{2,1,0:T(8,128)(2,1)}, u32[]{:S(2)}, u32[]{:S(2)}) collective-permute-start(s16[4,528,128]{2,1,0:T(8,128)(2,1)} %get-tuple-element.237), channel_id=1, source_target_pairs={{0,8},{8,0},{16,24},{24,16},{1,9},{9,1},{17,25},{25,17},{2,10},{10... | collective-permute-start | bytes 1622024 | tf_op jit(solution)/shard_map/ppermute | solution.py:332
  45.1 28.0 %collective-permute-start.37 = (s16[4,528,128]{2,1,0:T(8,128)(2,1)}, s16[4,528,128]{2,1,0:T(8,128)(2,1)}, u32[]{:S(2)}, u32[]{:S(2)}) collective-permute-start(s16[4,528,128]{2,1,0:T(8,128)(2,1)} %get-tuple-element.237), channel_id=1, source_target_pairs={{16,0},{24,8},{0,16},{8,24},{17,1},{25,9},{1,17},{9,25},{18,2},{26... | collective-permute-start | bytes 1622024 | tf_op jit(solution)/shard_map/ppermute | solution.py:336
  47.0 25.1 %collective-permute-start.40 = (s16[4,528,128]{2,1,0:T(8,128)(2,1)}, s16[4,528,128]{2,1,0:T(8,128)(2,1)}, u32[]{:S(2)}, u32[]{:S(2)}) collective-permute-start(s16[4,528,128]{2,1,0:T(8,128)(2,1)} %get-tuple-element.238), channel_id=1, source_target_pairs={{16,0},{24,8},{0,16},{8,24},{17,1},{25,9},{1,17},{9,25},{18,2},{26... | collective-permute-start | bytes 1622024 | tf_op jit(solution)/shard_map/ppermute | solution.py:336
  47.1 9.6 %collective-permute-start.24 = (bf16[128,1024]{1,0:T(8,128)(2,1)S(1)}, bf16[128,1024]{1,0:T(8,128)(2,1)S(1)}, u32[]{:S(2)}, u32[]{:S(2)}) collective-permute-start(bf16[128,1024]{1,0:T(8,128)(2,1)S(1)} %collective-permute-done.23), channel_id=1, source_target_pairs={{2,0},{3,1},{10,8},{11,9},{18,16},{19,17},{26,24},{27,25}} | collective-permute-start | bytes 786440 | tf_op jit(solution)/shard_map/ppermute | solution.py:315
  56.7 27.6 %collective-permute-start.27 = (bf16[384,1024]{1,0:T(8,128)(2,1)S(1)}, bf16[384,1024]{1,0:T(8,128)(2,1)S(1)}, u32[]{:S(2)}, u32[]{:S(2)}) collective-permute-start(bf16[384,1024]{1,0:T(8,128)(2,1)S(1)} %pad_maximum_fusion.2), channel_id=1, source_target_pairs={{0,1},{1,0},{2,3},{3,2},{4,5},{5,4},{6,7},{7,6},{8,9},{9,8},{10,11... | collective-permute-start | bytes 2359304 | tf_op jit(solution)/shard_map/ppermute | solution.py:318
  56.8 22.1 %collective-permute-start.39 = (s16[4,528,128]{2,1,0:T(8,128)(2,1)}, s16[4,528,128]{2,1,0:T(8,128)(2,1)}, u32[]{:S(2)}, u32[]{:S(2)}) collective-permute-start(s16[4,528,128]{2,1,0:T(8,128)(2,1)} %get-tuple-element.238), channel_id=1, source_target_pairs={{0,8},{8,0},{16,24},{24,16},{1,9},{9,1},{17,25},{25,17},{2,10},{10... | collective-permute-start | bytes 1622024 | tf_op jit(solution)/shard_map/ppermute | solution.py:332
  57.9 21.7 %collective-permute-start.38 = (s16[4,528,128]{2,1,0:T(8,128)(2,1)}, s16[4,528,128]{2,1,0:T(8,128)(2,1)}, u32[]{:S(2)}, u32[]{:S(2)}) collective-permute-start(s16[4,528,128]{2,1,0:T(8,128)(2,1)} %collective-permute-done.36), channel_id=1, source_target_pairs={{16,0},{24,8},{0,16},{8,24},{17,1},{25,9},{1,17},{9,25},{18,2},{26... | collective-permute-start | bytes 1622024 | tf_op jit(solution)/shard_map/ppermute | solution.py:336
  72.1 12.2 %collective-permute-start.41 = (s16[4,528,128]{2,1,0:T(8,128)(2,1)}, s16[4,528,128]{2,1,0:T(8,128)(2,1)}, u32[]{:S(2)}, u32[]{:S(2)}) collective-permute-start(s16[4,528,128]{2,1,0:T(8,128)(2,1)} %collective-permute-done.40), channel_id=1, source_target_pairs={{0,8},{8,0},{16,24},{24,16},{1,9},{9,1},{17,25},{25,17},{2,10},{10... | collective-permute-start | bytes 1622024 | tf_op jit(solution)/shard_map/ppermute | solution.py:332
  73.1 6.5 %collective-permute-start.20 = (bf16[128,1024]{1,0:T(8,128)(2,1)S(1)}, bf16[128,1024]{1,0:T(8,128)(2,1)S(1)}, u32[]{:S(2)}, u32[]{:S(2)}) collective-permute-start(bf16[128,1024]{1,0:T(8,128)(2,1)S(1)} %add.45), channel_id=1, source_target_pairs={{0,1},{1,0},{2,3},{3,2},{4,5},{5,4},{6,7},{7,6},{8,9},{9,8},{10,11... | collective-permute-start | bytes 786440 | tf_op jit(solution)/shard_map/ppermute | solution.py:318
  73.2 12.1 %copy-start.5 = (s32[16,8]{0,1:T(8,128)S(1)}, s32[16,8]{0,1:T(8,128)}, u32[]{:S(2)}) copy-start(s32[16,8]{0,1:T(8,128)} %param.12) | copy-start | bytes 1540
  73.2 12.1 %copy-start.18 = (bf16[8,128,128]{2,1,0:T(8,128)(2,1)S(1)}, bf16[8,128,128]{2,1,0:T(8,128)(2,1)}, u32[]{:S(2)}) copy-start(bf16[8,128,128]{2,1,0:T(8,128)(2,1)} %param.11) | copy-start | bytes 786436
  78.9 22.6 %collective-permute-start.12 = (s16[4,528,128]{2,1,0:T(8,128)(2,1)}, s16[4,528,128]{2,1,0:T(8,128)(2,1)}, u32[]{:S(2)}, u32[]{:S(2)}) collective-permute-start(s16[4,528,128]{2,1,0:T(8,128)(2,1)} %get-tuple-element.233), channel_id=1, source_target_pairs={{0,8},{8,0},{16,24},{24,16},{1,9},{9,1},{17,25},{25,17},{2,10},{10... | collective-permute-start | bytes 1622024 | tf_op jit(solution)/shard_map/ppermute | solution.py:332
  84.4 0.9 copy-start.7
  85.3 29.6 %copy-start = (bf16[128,4096]{1,0:T(8,128)(2,1)S(1)}, bf16[128,4096]{1,0:T(8,128)(2,1)}, u32[]{:S(2)}) copy-start(bf16[128,4096]{1,0:T(8,128)(2,1)} %refs_0_.7) | copy-start | bytes 3145732
  98.1 15.4 %collective-permute-start.16 = (s16[4,528,128]{2,1,0:T(8,128)(2,1)}, s16[4,528,128]{2,1,0:T(8,128)(2,1)S(1)}, u32[]{:S(2)}, u32[]{:S(2)}) collective-permute-start(s16[4,528,128]{2,1,0:T(8,128)(2,1)} %get-tuple-element.234), channel_id=1, source_target_pairs={{16,0},{24,8},{0,16},{8,24},{17,1},{25,9},{1,17},{9,25},{18,2},{26... | collective-permute-start | bytes 1622024 | tf_op jit(solution)/shard_map/ppermute | solution.py:336
  100.0 25.1 %collective-permute-start.13 = (s16[4,528,128]{2,1,0:T(8,128)(2,1)}, s16[4,528,128]{2,1,0:T(8,128)(2,1)S(1)}, u32[]{:S(2)}, u32[]{:S(2)}) collective-permute-start(s16[4,528,128]{2,1,0:T(8,128)(2,1)} %get-tuple-element.233), channel_id=1, source_target_pairs={{16,0},{24,8},{0,16},{8,24},{17,1},{25,9},{1,17},{9,25},{18,2},{26... | collective-permute-start | bytes 1622024 | tf_op jit(solution)/shard_map/ppermute | solution.py:336
  100.2 24.9 %collective-permute-start.15 = (s16[4,528,128]{2,1,0:T(8,128)(2,1)}, s16[4,528,128]{2,1,0:T(8,128)(2,1)S(1)}, u32[]{:S(2)}, u32[]{:S(2)}) collective-permute-start(s16[4,528,128]{2,1,0:T(8,128)(2,1)} %get-tuple-element.234), channel_id=1, source_target_pairs={{0,8},{8,0},{16,24},{24,16},{1,9},{9,1},{17,25},{25,17},{2,10},{10... | collective-permute-start | bytes 1622024 | tf_op jit(solution)/shard_map/ppermute | solution.py:332
  101.6 30.3 %collective-permute-start.14 = (s16[4,528,128]{2,1,0:T(8,128)(2,1)}, s16[4,528,128]{2,1,0:T(8,128)(2,1)S(1)}, u32[]{:S(2)}, u32[]{:S(2)}) collective-permute-start(s16[4,528,128]{2,1,0:T(8,128)(2,1)} %collective-permute-done.12), channel_id=1, source_target_pairs={{16,0},{24,8},{0,16},{8,24},{17,1},{25,9},{1,17},{9,25},{18,2},{26... | collective-permute-start | bytes 1622024 | tf_op jit(solution)/shard_map/ppermute | solution.py:336
  113.5 18.4 %collective-permute-start.17 = (s16[4,528,128]{2,1,0:T(8,128)(2,1)S(1)}, s16[4,528,128]{2,1,0:T(8,128)(2,1)S(1)}, u32[]{:S(2)}, u32[]{:S(2)}) collective-permute-start(s16[4,528,128]{2,1,0:T(8,128)(2,1)S(1)} %collective-permute-done.16), channel_id=1, source_target_pairs={{0,8},{8,0},{16,24},{24,16},{1,9},{9,1},{17,25},{25,17},{2,10},{10... | collective-permute-start | bytes 1622024 | tf_op jit(solution)/shard_map/ppermute | solution.py:332
  116.0 42.5 %collective-permute-start.42 = (bf16[128,2048]{1,0:T(8,128)(2,1)}, bf16[128,2048]{1,0:T(8,128)(2,1)S(1)}, u32[]{:S(2)}, u32[]{:S(2)}) collective-permute-start(bf16[128,2048]{1,0:T(8,128)(2,1)} %get-tuple-element.388), channel_id=1, source_target_pairs={{0,2},{1,3},{2,4},{3,5},{4,6},{5,7},{8,10},{9,11},{10,12},{11,13},... | collective-permute-start | bytes 1572872 | tf_op jit(solution)/shard_map/ppermute | solution.py:311
  131.9 0.8 copy-start.8
  135.1 0.8 copy-start.16
  148.8 18.9 %collective-permute-start.43 = (bf16[128,2048]{1,0:T(8,128)(2,1)}, bf16[128,2048]{1,0:T(8,128)(2,1)}, u32[]{:S(2)}, u32[]{:S(2)}) collective-permute-start(bf16[128,2048]{1,0:T(8,128)(2,1)} %get-tuple-element.388), channel_id=1, source_target_pairs={{2,0},{3,1},{4,2},{5,3},{6,4},{7,5},{10,8},{11,9},{12,10},{13,11},... | collective-permute-start | bytes 1572872 | tf_op jit(solution)/shard_map/ppermute | solution.py:315
  150.1 28.9 %collective-permute-start.30 = (bf16[128,2048]{1,0:T(8,128)(2,1)}, bf16[128,2048]{1,0:T(8,128)(2,1)}, u32[]{:S(2)}, u32[]{:S(2)}) collective-permute-start(bf16[128,2048]{1,0:T(8,128)(2,1)} %get-tuple-element.389), channel_id=1, source_target_pairs={{2,0},{3,1},{4,2},{5,3},{6,4},{7,5},{10,8},{11,9},{12,10},{13,11},... | collective-permute-start | bytes 1572872 | tf_op jit(solution)/shard_map/ppermute | solution.py:315
  151.4 28.9 %collective-permute-start.29 = (bf16[128,2048]{1,0:T(8,128)(2,1)}, bf16[128,2048]{1,0:T(8,128)(2,1)S(1)}, u32[]{:S(2)}, u32[]{:S(2)}) collective-permute-start(bf16[128,2048]{1,0:T(8,128)(2,1)} %get-tuple-element.389), channel_id=1, source_target_pairs={{0,2},{1,3},{2,4},{3,5},{4,6},{5,7},{8,10},{9,11},{10,12},{11,13},... | collective-permute-start | bytes 1572872 | tf_op jit(solution)/shard_map/ppermute | solution.py:311
  158.5 23.2 %collective-permute-start.46 = (bf16[128,2048]{1,0:T(8,128)(2,1)S(1)}, bf16[128,2048]{1,0:T(8,128)(2,1)}, u32[]{:S(2)}, u32[]{:S(2)}) collective-permute-start(bf16[128,2048]{1,0:T(8,128)(2,1)S(1)} %collective-permute-done.42), channel_id=1, source_target_pairs={{2,4},{3,5},{4,6},{5,7},{10,12},{11,13},{12,14},{13,15},{18,20},{1... | collective-permute-start | bytes 1572872 | tf_op jit(solution)/shard_map/ppermute | solution.py:311
  167.7 22.5 %collective-permute-start.44 = (bf16[128,2048]{1,0:T(8,128)(2,1)}, bf16[128,2048]{1,0:T(8,128)(2,1)}, u32[]{:S(2)}, u32[]{:S(2)}) collective-permute-start(bf16[128,2048]{1,0:T(8,128)(2,1)} %collective-permute-done.43), channel_id=1, source_target_pairs={{2,0},{3,1},{4,2},{5,3},{10,8},{11,9},{12,10},{13,11},{18,16},{19,... | collective-permute-start | bytes 1572872 | tf_op jit(solution)/shard_map/ppermute | solution.py:315
  169.0 53.3 %collective-permute-start.28 = (bf16[128,4096]{1,0:T(8,128)(2,1)S(1)}, bf16[128,4096]{1,0:T(8,128)(2,1)S(1)}, u32[]{:S(2)}, u32[]{:S(2)}) collective-permute-start(bf16[128,4096]{1,0:T(8,128)(2,1)S(1)} %copy-done), channel_id=1, source_target_pairs={{0,1},{1,0},{2,3},{3,2},{4,5},{5,4},{6,7},{7,6},{8,9},{9,8},{10,11... | collective-permute-start | bytes 3145736 | tf_op jit(solution)/shard_map/ppermute | solution.py:318
  178.9 22.5 %collective-permute-start.31 = (bf16[128,2048]{1,0:T(8,128)(2,1)}, bf16[128,2048]{1,0:T(8,128)(2,1)}, u32[]{:S(2)}, u32[]{:S(2)}) collective-permute-start(bf16[128,2048]{1,0:T(8,128)(2,1)} %collective-permute-done.30), channel_id=1, source_target_pairs={{2,0},{3,1},{4,2},{5,3},{10,8},{11,9},{12,10},{13,11},{18,16},{19,... | collective-permute-start | bytes 1572872 | tf_op jit(solution)/shard_map/ppermute | solution.py:315
  180.2 12.3 %collective-permute-start.33 = (bf16[128,2048]{1,0:T(8,128)(2,1)S(1)}, bf16[128,2048]{1,0:T(8,128)(2,1)}, u32[]{:S(2)}, u32[]{:S(2)}) collective-permute-start(bf16[128,2048]{1,0:T(8,128)(2,1)S(1)} %collective-permute-done.29), channel_id=1, source_target_pairs={{2,4},{3,5},{4,6},{5,7},{10,12},{11,13},{12,14},{13,15},{18,20},{1... | collective-permute-start | bytes 1572872 | tf_op jit(solution)/shard_map/ppermute | solution.py:311
  181.7 21.2 %collective-permute-start.47 = (bf16[128,2048]{1,0:T(8,128)(2,1)}, bf16[128,2048]{1,0:T(8,128)(2,1)}, u32[]{:S(2)}, u32[]{:S(2)}) collective-permute-start(bf16[128,2048]{1,0:T(8,128)(2,1)} %collective-permute-done.46), channel_id=1, source_target_pairs={{4,6},{5,7},{12,14},{13,15},{20,22},{21,23},{28,30},{29,31}} | collective-permute-start | bytes 1572872 | tf_op jit(solution)/shard_map/ppermute | solution.py:311
  190.2 22.4 %collective-permute-start.45 = (bf16[128,2048]{1,0:T(8,128)(2,1)}, bf16[128,2048]{1,0:T(8,128)(2,1)S(1)}, u32[]{:S(2)}, u32[]{:S(2)}) collective-permute-start(bf16[128,2048]{1,0:T(8,128)(2,1)} %collective-permute-done.44), channel_id=1, source_target_pairs={{2,0},{3,1},{10,8},{11,9},{18,16},{19,17},{26,24},{27,25}} | collective-permute-start | bytes 1572872 | tf_op jit(solution)/shard_map/ppermute | solution.py:315
  192.6 21.8 %collective-permute-start.34 = (bf16[128,2048]{1,0:T(8,128)(2,1)}, bf16[128,2048]{1,0:T(8,128)(2,1)S(1)}, u32[]{:S(2)}, u32[]{:S(2)}) collective-permute-start(bf16[128,2048]{1,0:T(8,128)(2,1)} %collective-permute-done.33), channel_id=1, source_target_pairs={{4,6},{5,7},{12,14},{13,15},{20,22},{21,23},{28,30},{29,31}} | collective-permute-start | bytes 1572872 | tf_op jit(solution)/shard_map/ppermute | solution.py:311
  201.4 19.6 %collective-permute-start.32 = (bf16[128,2048]{1,0:T(8,128)(2,1)}, bf16[128,2048]{1,0:T(8,128)(2,1)S(1)}, u32[]{:S(2)}, u32[]{:S(2)}) collective-permute-start(bf16[128,2048]{1,0:T(8,128)(2,1)} %collective-permute-done.31), channel_id=1, source_target_pairs={{2,0},{3,1},{10,8},{11,9},{18,16},{19,17},{26,24},{27,25}} | collective-permute-start | bytes 1572872 | tf_op jit(solution)/shard_map/ppermute | solution.py:315
  212.8 8.3 %copy-start.2 = (bf16[384,2048]{1,0:T(8,128)(2,1)}, bf16[384,2048]{1,0:T(8,128)(2,1)S(1)}, u32[]{:S(2)}) copy-start(bf16[384,2048]{1,0:T(8,128)(2,1)S(1)} %pad_maximum_fusion.1.refs_2_) | copy-start | bytes 4718596
  212.8 9.5 %collective-permute-start.48 = (bf16[384,2048]{1,0:T(8,128)(2,1)S(1)}, bf16[384,2048]{1,0:T(8,128)(2,1)S(1)}, u32[]{:S(2)}, u32[]{:S(2)}) collective-permute-start(bf16[384,2048]{1,0:T(8,128)(2,1)S(1)} %pad_maximum_fusion.1.refs_2_), channel_id=1, source_target_pairs={{0,1},{1,0},{2,3},{3,2},{4,5},{5,4},{6,7},{7,6},{8,9},{9,8},{10,11... | collective-permute-start | bytes 4718600 | tf_op jit(solution)/shard_map/ppermute | solution.py:318
  222.3 35.4 %collective-permute-start.35 = (bf16[384,2048]{1,0:T(8,128)(2,1)}, bf16[384,2048]{1,0:T(8,128)(2,1)}, u32[]{:S(2)}, u32[]{:S(2)}) collective-permute-start(bf16[384,2048]{1,0:T(8,128)(2,1)} %pad_maximum_fusion.refs_2_), channel_id=1, source_target_pairs={{0,1},{1,0},{2,3},{3,2},{4,5},{5,4},{6,7},{7,6},{8,9},{9,8},{10,11... | collective-permute-start | bytes 4718600 | tf_op jit(solution)/shard_map/ppermute | solution.py:318
  222.3 1.5 copy-start.1
  222.3 1.2 copy-start.4
  240.7 17.0 %copy-start.3 = (bf16[1024,1024]{1,0:T(8,128)(2,1)S(1)}, bf16[1024,1024]{1,0:T(8,128)(2,1)}, u32[]{:S(2)}) copy-start(bf16[1024,1024]{1,0:T(8,128)(2,1)} %get-tuple-element.239.hi_ref) | copy-start | bytes 6291460
  (3 other events, 2.4 us)
